TPU v7x, 32 devices: a whole 2x2x4 slice. The times are simulated.
32 devices in a mesh: tm: 4 (over x, core), space: 8 (over z, y).
Axes of the slice: x: 2, y: 2, z: 4, core: 2. Of those that a mesh axis runs over, the one named last changes fastest.
Arguments:
- cotangent: bfloat16 [16, 64, 8192], P('tm', 'space'), may hold values from -6 to 6
- saved_mix: bfloat16 [16, 64, 8192], P('tm', 'space'), may hold values from -6 to 6
- saved_pre: bfloat16 [16, 64, 8192], P('tm', 'space'), may hold values from -8 to 8
- kernel_one: bfloat16 [4, 3, 3, 64, 64], replicated, may hold values from -0.25 to 0.25
- kernel_two: bfloat16 [4, 3, 3, 64, 64], replicated, may hold values from -0.25 to 0.25
- ref_pairs: int32 [16, 2], replicated, may hold values from 0 to 15, as said below
- frame_level: int32 [16], replicated, may hold values from 0 to 4, as said below
Outputs:
- input_grad: float32 [16, 64, 8192], P('tm', 'space')
- weight_grad_one: float32 [4, 3, 3, 64, 64], replicated
- weight_grad_two: float32 [4, 3, 3, 64, 64], replicated
Inputs may be any that keep to these rules, and one draw needn't show every extreme that they name: Frame c was predicted from frames ref_pairs[c, 0] and ref_pairs[c, 1]; for a frame of level k >= 1 both have a level below k (at level 1 both name the level-0 frame); the level-0 frame names itself twice. `frame_level`: one frame has level 0 and 2**(k-1) frames have level k for k from 1 to 4; frames are stored in an order drawn from the seed.
All inputs are finite; a program needn't handle non-finite values.
Results may differ from a plain program's by a relative error of at most 0.006.
Values may be sent and summed in bfloat16 or wider, within the bound.
A program may use at most 64 MiB of HBM per device.

v0:
```python
import math
import jax
import jax.numpy as jnp
from jax import lax
from jax.sharding import PartitionSpec as P


def padded_2(cells, sides, width):
    for axis, dim in sides:
        count = lax.axis_size(axis)
        ends = count - 1
        head = lax.slice_in_dim(cells, 0, width, axis=dim)
        tail = lax.slice_in_dim(cells, cells.shape[dim] - width, cells.shape[dim], axis=dim)
        cells = jnp.concatenate(
            [
                lax.ppermute(tail, axis, [(i, (i + 1) % count) for i in range(ends)]),
                cells,
                lax.ppermute(head, axis, [((i + 1) % count, i) for i in range(ends)]),
            ],
            axis=dim,
        )
    return cells


def flipped(kernel):
    return jnp.transpose(kernel[::-1, ::-1], (0, 1, 3, 2))


def pair_kernel(kernel):
    blank = jnp.zeros_like(kernel[:, 0])
    row_blocks = []
    for in_part in range(4):
        col_blocks = []
        for out_half in range(2):
            col_tap = in_part - out_half
            col_blocks.append(kernel[:, col_tap] if 0 <= col_tap <= 2 else blank)
        row_blocks.append(jnp.concatenate(col_blocks, axis=-1))
    return jnp.concatenate(row_blocks, axis=1)


def pair_view(field, channels):
    col_count = field.shape[2] // channels
    grid = field.reshape(field.shape[0], field.shape[1], col_count, channels)
    grid = jnp.pad(grid, ((0, 0), (0, 0), (1, 1), (0, 0)))
    grid = grid.reshape(field.shape[0], field.shape[1], (col_count + 2) // 2, 2 * channels)
    return jnp.concatenate((grid[:, :, :-1], grid[:, :, 1:]), axis=-1)


def conv_taps(field, paired):
    channels = paired.shape[2] // 2
    windows = pair_view(field, channels)
    row_count = field.shape[1] - 2
    result = jnp.einsum(
        "nrjk,kc->nrjc", windows[:, 0:row_count], paired[0], preferred_element_type=jnp.float32
    )
    for row_tap in range(1, 3):
        result = result + jnp.einsum(
            "nrjk,kc->nrjc",
            windows[:, row_tap : row_tap + row_count],
            paired[row_tap],
            preferred_element_type=jnp.float32,
        )
    return result.reshape(field.shape[0], row_count, -1)


def correlate(field, cot, channels):
    windows = pair_view(field, channels)
    row_count = cot.shape[1]
    cot_pairs = cot.reshape(cot.shape[0], row_count, -1, 2 * channels)
    taps = []
    for row_tap in range(3):
        blocks = jnp.einsum(
            "nrjk,nrjc->nkc",
            windows[:, row_tap : row_tap + row_count],
            cot_pairs,
            preferred_element_type=jnp.float32,
        )
        row_taps = []
        for col_tap in range(3):
            first_part = blocks[:, col_tap * channels : (col_tap + 1) * channels, 0:channels]
            second_part = blocks[
                :, (col_tap + 1) * channels : (col_tap + 2) * channels, channels : 2 * channels
            ]
            row_taps.append(first_part + second_part)
        taps.append(jnp.stack(row_taps, axis=1))
    return jnp.stack(taps, axis=1)


def backprop(slot_cot, slot_slope, kernel_inner, kernel_outer):
    padded = padded_2(slot_cot, (("space", 1),), 1)
    slot_grad = (conv_taps(padded, kernel_inner) * slot_slope).astype(jnp.bfloat16)
    grad_padded = padded_2(slot_grad, (("space", 1),), 1)
    to_refs = conv_taps(grad_padded, kernel_outer).astype(jnp.bfloat16)
    return (slot_grad, to_refs)


def body_time(cotangent, saved_mix, saved_pre, kernel_one, kernel_two, ref_pairs, frame_level):
    frames_dev = cotangent.shape[0]
    row_count = cotangent.shape[1]
    channels = kernel_one.shape[-1]
    levels_all = kernel_one.shape[0]
    col_count = cotangent.shape[2] // channels
    first_frame = lax.axis_index("tm") * frames_dev
    local_ids = first_frame + jnp.arange(frames_dev, dtype=jnp.int32)
    local_level = lax.dynamic_slice_in_dim(frame_level, first_frame, frames_dev, 0)
    frame_count = ref_pairs.shape[0]
    all_frames = jnp.arange(frame_count, dtype=jnp.int32)
    preact = saved_pre.astype(jnp.float32)
    sigmoid_pre = jax.nn.sigmoid(preact)
    act_slope = sigmoid_pre * (1.0 + preact * (1.0 - sigmoid_pre))
    act_out = (preact * sigmoid_pre).astype(jnp.bfloat16)
    saved_rims = padded_2(jnp.stack((saved_mix, act_out)), (("space", 2),), 1)
    cot_total = cotangent.astype(jnp.float32)
    kept_grad = jnp.zeros_like(cotangent)
    for level_now in range(levels_all, 0, -1):
        active = local_level == level_now
        slot_count = min(frames_dev, 2 ** (level_now - 1))
        ranks = jnp.cumsum(active.astype(jnp.int32)) - 1
        picker = jnp.logical_and(
            ranks[None, :] == jnp.arange(slot_count, dtype=jnp.int32)[:, None], active[None, :]
        )
        picker_wide = picker.astype(jnp.float32)
        slot_cot = jnp.einsum(
            "sf,fx->sx",
            picker.astype(jnp.bfloat16),
            cot_total.astype(jnp.bfloat16).reshape(frames_dev, -1),
            preferred_element_type=jnp.float32,
        )
        slot_cot = slot_cot.astype(jnp.bfloat16).reshape(slot_count, row_count, -1)
        slot_slope = jnp.einsum(
            "sf,fx->sx",
            picker_wide,
            act_slope.reshape(frames_dev, -1),
            precision=lax.Precision.HIGHEST,
        ).reshape(slot_count, row_count, -1)
        slot_ids = jnp.sum(picker.astype(jnp.int32) * local_ids[None, :], axis=1)
        slot_ok = jnp.sum(picker.astype(jnp.int32), axis=1)
        kernel_inner = pair_kernel(flipped(kernel_two[level_now - 1]))
        kernel_outer = pair_kernel(flipped(kernel_one[level_now - 1]))
        slot_grad, to_refs = backprop(slot_cot, slot_slope, kernel_inner, kernel_outer)
        frame_grad = jnp.einsum(
            "sf,sx->fx",
            picker.astype(jnp.bfloat16),
            slot_grad.reshape(slot_grad.shape[0], -1),
            preferred_element_type=jnp.float32,
        )
        frame_grad = frame_grad.astype(jnp.bfloat16).reshape(kept_grad.shape)
        kept_grad = jnp.where(active[:, None, None], frame_grad, kept_grad)
        moved = lax.all_gather(to_refs, "tm", axis=0, tiled=True)
        sender_ids = lax.all_gather(slot_ids, "tm", axis=0, tiled=True)
        sender_ok = lax.all_gather(slot_ok, "tm", axis=0, tiled=True)
        matches = (sender_ids[:, None] == all_frames[None, :]).astype(jnp.int32)
        first_ref = jnp.sum(matches * ref_pairs[None, :, 0], axis=1)
        second_ref = jnp.sum(matches * ref_pairs[None, :, 1], axis=1)
        hits = (first_ref[:, None] == local_ids[None, :]).astype(jnp.float32) + (
            second_ref[:, None] == local_ids[None, :]
        ).astype(jnp.float32)
        weights = 0.5 * sender_ok[:, None].astype(jnp.float32) * hits
        added = jnp.einsum(
            "kf,kx->fx",
            weights.astype(jnp.bfloat16),
            moved.reshape(moved.shape[0], -1),
            preferred_element_type=jnp.float32,
        )
        cot_total = cot_total + added.reshape(cot_total.shape)
    final_cot = cot_total.astype(jnp.bfloat16)
    per_one = correlate(saved_rims[0], kept_grad, channels)
    per_two = correlate(saved_rims[1], final_cot, channels)
    level_hot = (
        local_level[:, None] == jnp.arange(1, levels_all + 1, dtype=jnp.int32)[None, :]
    ).astype(jnp.float32)
    scale = 1.0 / math.sqrt(row_count * lax.axis_size("space") * col_count)
    sum_one = scale * jnp.sum(level_hot[:, :, None, None, None, None] * per_one[:, None], axis=0)
    sum_two = scale * jnp.sum(level_hot[:, :, None, None, None, None] * per_two[:, None], axis=0)
    weight_one, weight_two = lax.psum((sum_one, sum_two), ("tm", "space"))
    return (cot_total, weight_one, weight_two)


def on_device(cotangent, saved_mix, saved_pre, kernel_one, kernel_two, ref_pairs, frame_level):
    return body_time(
        cotangent, saved_mix, saved_pre, kernel_one, kernel_two, ref_pairs, frame_level
    )


def solution(mesh):
    placed = (
        P("tm", "space", None),
        P("tm", "space", None),
        P("tm", "space", None),
        P(),
        P(),
        P(),
        P(),
    )
    return jax.shard_map(
        on_device,
        mesh=mesh,
        in_specs=placed,
        out_specs=(P("tm", "space", None), P(), P()),
        check_vma=False,
    )
```

profile of v0, /device:TPU:0, one launch (start us, length us, event | category | flops | bytes accessed | tf_op | source)
XLA Modules:
  0.0 384.8 jit_solution(5619695112859020218)
XLA Ops:
  7.2 1.3 broadcast_compare_fusion
  10.0 1.4 copy.215
  13.1 4.9 %collective-permute-start = (bf16[4,1,8192]{2,0,1:T(4,128)(2,1)S(1)}, bf16[4,1,8192]{2,0,1:T(4,128)(2,1)S(1)}, u32[]{:S(2)}, u32[]{:S(2)}) collective-permute-start(bf16[4,1,8192]{2,0,1:T(4,128)(2,1)S(1)} %get-tuple-element.102), channel_id=1, source_target_pairs={{0,1},{1,2},{2,3},{3,4},{4,5},{5,6},{6,7},{8,9},{9,10},{10,11},{11... | collective-permute-start | bytes 196616 | tf_op jit(solution)/shard_map/ppermute | solution.py:16
  18.0 1.3 collective-permute-start.1
  21.1 2.3 fusion.46
  27.4 1.4 select_maximum_fusion.2
  32.2 2.4 fusion
  34.6 4.6 %collective-permute-start.2 = (bf16[4,1,8192]{2,0,1:T(4,128)(2,1)S(1)}, bf16[4,1,8192]{2,0,1:T(4,128)(2,1)S(1)}, u32[]{:S(2)}, u32[]{:S(2)}) collective-permute-start(bf16[4,1,8192]{2,0,1:T(4,128)(2,1)S(1)} %get-tuple-element.100), channel_id=1, source_target_pairs={{0,1},{1,2},{2,3},{3,4},{4,5},{5,6},{6,7},{8,9},{9,10},{10,11},{11... | collective-permute-start | bytes 196616 | tf_op jit(solution)/shard_map/ppermute | solution.py:16
  39.2 1.5 collective-permute-start.3
  41.0 4.7 %collective-permute-done.3 = bf16[4,1,8192]{2,0,1:T(4,128)(2,1)S(1)} collective-permute-done((bf16[4,1,8192]{2,0,1:T(4,128)(2,1)S(1)}, bf16[4,1,8192]{2,0,1:T(4,128)(2,1)S(1)}, u32[]{:S(2)}, u32[]{:S(2)}) %collective-permute-start.3) | collective-permute-done | bytes 65568 | tf_op jit(solution)/shard_map/ppermute | solution.py:18
  46.2 1.9 reshape.439
  48.2 1.8 pad.50
  53.8 1.3 pad_maximum_fusion.21
  55.1 5.7 %collective-permute-start.16 = (bf16[2,4,1,8192]{3,2,1,0:T(2,128)(2,1)}, bf16[2,4,1,8192]{3,2,1,0:T(2,128)(2,1)}, u32[]{:S(2)}, u32[]{:S(2)}) collective-permute-start(bf16[2,4,1,8192]{3,2,1,0:T(2,128)(2,1)} %get-tuple-element.54), channel_id=1, source_target_pairs={{0,1},{1,2},{2,3},{3,4},{4,5},{5,6},{6,7},{8,9},{9,10},{10,11},{11... | collective-permute-start | bytes 393224 | tf_op jit(solution)/shard_map/ppermute | solution.py:16
  60.8 1.3 collective-permute-start.17
  66.2 1.5 dynamic-update-slice.6
  67.7 1.4 dynamic-update-slice.7
  69.0 5.7 %all-reduce.34 = (s32[16]{0:T(128)S(1)}, s32[16]{0:T(128)S(1)}, s32[16]{0:T(128)S(1)}, s32[16]{0:T(128)}, s32[8]{0:T(128)S(1)}, /*index=5*/s32[8]{0:T(128)}, s32[4]{0:T(128)S(1)}, s32[4]{0:T(128)}) all-reduce(s32[16]{0:T(128)S(1)} %dynamic-update-slice.3, s32[16]{0:T(128)S(1)} %dynamic-update-slice.1, ...), channel_id=1, replica_groups=mesh['tm'=4,'space'=8] {'tm'}, use_global_device_ids=true, to_apply=%add.29 | all-reduce | flops 88 | bytes 704
  75.8 2.2 all-gather.4.cloned.1.call-done
  78.1 5.5 %fusion.214 = (bf16[4,8,8192]{2,0,1:T(4,128)(2,1)S(1)}, f32[4,8,8192]{2,0,1:T(4,128)}) fusion(s32[16]{0:T(128)S(1)} %get-tuple-element.31, s32[16]{0:T(128)S(1)} %get-tuple-element.30, f32[16]{0:T(128)S(1)} %convert_multiply_fusion.5, s32[4]{0:T(128)S(1)} %get-tuple-element.160, bf16[4,8,8192]{2,1,0:T(8,128)(2,1)S(1)} %copy-done.31, ...), kind=kOutput, calls=%fused_computation.415 | convolution fusion | flops 9175488 | bytes 4194512 | tf_op jit(solution)/shard_map/kf,kx->fx/dot_general | solution.py:159
  84.2 3.4 collective-permute-start.4
  87.6 1.7 collective-permute-start.5
  91.7 2.0 collective-permute-done.5
  94.5 1.4 select_maximum_fusion
  99.3 2.4 fusion.1
  101.7 4.3 %collective-permute-start.6 = (bf16[4,1,8192]{2,0,1:T(4,128)(2,1)S(1)}, bf16[4,1,8192]{2,0,1:T(4,128)(2,1)S(1)}, u32[]{:S(2)}, u32[]{:S(2)}) collective-permute-start(bf16[4,1,8192]{2,0,1:T(4,128)(2,1)S(1)} %get-tuple-element.96), channel_id=1, source_target_pairs={{0,1},{1,2},{2,3},{3,4},{4,5},{5,6},{6,7},{8,9},{9,10},{10,11},{11... | collective-permute-start | bytes 196616 | tf_op jit(solution)/shard_map/ppermute | solution.py:16
  106.0 1.3 collective-permute-start.7
  107.9 4.3 %collective-permute-done.7 = bf16[4,1,8192]{2,0,1:T(4,128)(2,1)S(1)} collective-permute-done((bf16[4,1,8192]{2,0,1:T(4,128)(2,1)S(1)}, bf16[4,1,8192]{2,0,1:T(4,128)(2,1)S(1)}, u32[]{:S(2)}, u32[]{:S(2)}) %collective-permute-start.7) | collective-permute-done | bytes 65568 | tf_op jit(solution)/shard_map/ppermute | solution.py:18
  112.7 1.9 reshape.447
  114.6 1.8 pad.52
  124.9 2.4 fusion.143
  127.2 15.2 %all-gather.6.cloned.1.call-done = bf16[16,8,8192]{2,1,0:T(8,128)(2,1)} async-done(((bf16[4,8,8192]{2,1,0:T(8,128)(2,1)}), bf16[16,8,8192]{2,1,0:T(8,128)(2,1)}) %all-gather.6.cloned.1.call-update) | async-done | bytes 2097168 | tf_op jit(solution)/shard_map/all_gather | solution.py:149
  142.4 5.2 %fusion.215 = (bf16[4,8,8192]{2,0,1:T(4,128)(2,1)S(1)}, f32[4,8,8192]{2,0,1:T(4,128)}) fusion(f32[4,8,8192]{2,0,1:T(4,128)S(1)} %copy-done.14, s32[16]{0:T(128)S(1)} %get-tuple-element.32, s32[16]{0:T(128)S(1)} %get-tuple-element.29, f32[16]{0:T(128)S(1)} %convert_multiply_fusion.4, s32[4]{0:T(128)S(1)} %get-tuple-element.160, ...), kind=kOutput, calls=%fused_computation.416 | convolution fusion | flops 8913344 | bytes 4718800 | tf_op jit(solution)/shard_map/kf,kx->fx/dot_general | solution.py:159
  148.1 3.4 collective-permute-start.8
  151.5 1.3 collective-permute-start.9
  154.5 2.7 collective-permute-done.9
  159.3 2.0 fusion.2
  161.3 4.3 %collective-permute-start.10 = (bf16[2,1,8192]{2,0,1:T(2,128)(2,1)S(1)}, bf16[2,1,8192]{2,0,1:T(2,128)(2,1)S(1)}, u32[]{:S(2)}, u32[]{:S(2)}) collective-permute-start(bf16[2,1,8192]{2,0,1:T(2,128)(2,1)S(1)} %get-tuple-element.108), channel_id=1, source_target_pairs={{0,1},{1,2},{2,3},{3,4},{4,5},{5,6},{6,7},{8,9},{9,10},{10,11},{11... | collective-permute-start | bytes 98312 | tf_op jit(solution)/shard_map/ppermute | solution.py:16
  165.6 1.5 collective-permute-start.11
  167.1 2.0 pad_maximum_fusion
  169.1 2.2 collective-permute-done.11
  171.9 1.3 reshape.455
  173.2 1.3 pad.54
  176.8 1.1 fusion.193
  178.5 1.1 reshape_squeeze.7
  181.8 1.9 reshape_squeeze.6
  183.7 1.8 pad.57
  186.3 1.3 fusion.195
  187.6 1.3 fusion.194
  189.4 3.3 all-gather.8.cloned.1.call-done
  192.7 2.7 fusion.216
  196.0 3.4 collective-permute-start.12
  199.4 1.5 collective-permute-start.13
  201.9 3.3 collective-permute-done.13
  211.1 4.3 %collective-permute-start.14 = (bf16[1,1,8192]{2,1,0:T(2,128)(2,1)S(1)}, bf16[1,1,8192]{2,1,0:T(2,128)(2,1)S(1)}, u32[]{:S(2)}, u32[]{:S(2)}) collective-permute-start(bf16[1,1,8192]{2,1,0:T(2,128)(2,1)S(1)} %get-tuple-element.140), channel_id=1, source_target_pairs={{0,1},{1,2},{2,3},{3,4},{4,5},{5,6},{6,7},{8,9},{9,10},{10,11},{11... | collective-permute-start | bytes 49160 | tf_op jit(solution)/shard_map/ppermute | solution.py:16
  215.4 1.3 collective-permute-start.15
  218.5 2.7 collective-permute-done.15
  222.6 6.5 %all_gather.47 = bf16[4,8,8192]{2,1,0:T(8,128)(2,1)S(1)} all-gather(bf16[1,8,8192]{2,1,0:T(8,128)(2,1)S(1)} %convert_element_type.244), channel_id=1, replica_groups=mesh['tm'=4,'space'=8] {'tm'}, dimensions={0}, use_global_device_ids=true | all-gather | bytes 655360 | tf_op jit(solution)/shard_map/all_gather | solution.py:149
  230.6 1.8 convolution_bitcast_fusion.2
  236.2 1.2 broadcast_multiply_fusion
  237.4 1.2 broadcast_multiply_fusion.1
  238.6 1.6 copy.155
  240.2 134.1 %all-reduce.38.cloned.1.call-done = (f32[4,3,3,64,64]{4,3,2,1,0:T(8,128)}, f32[4,3,3,64,64]{4,3,2,1,0:T(8,128)}) async-done(((f32[4,3,3,64,64]{4,3,2,1,0:T(8,128)}, f32[4,3,3,64,64]{4,3,2,1,0:T(8,128)}), (f32[4,3,3,64,64]{4,3,2,1,0:T(8,128)}, f32[4,3,3,64,64]{4,3,2,1,0:T(8,128)})) %all-reduce.38.cloned.1.call-update) | async-done | bytes 1179664 | tf_op jit(solution)/shard_map/psum | solution.py:175
  374.3 2.5 copy.332
  (337 shorter events, 64.5 us)
Async XLA Ops:
  7.2 70.9 %all-gather.4.cloned.1.call-start = ((), (), s32[]{:S(2)}) async-start(), calls=%async_computation | async-start | bytes 2621440 | tf_op jit(solution)/shard_map/all_gather | solution.py:149
  8.5 4.0 %copy-start.45 = (s32[4]{0:T(128)}, s32[4]{0:T(128)S(1)}, u32[]{:S(2)}) copy-start(s32[4]{0:T(128)S(1)} %get-tuple-element.44) | copy-start | bytes 52
  9.2 3.2 copy-start.41
  9.3 3.2 copy-start.43
  9.3 56.3 %copy-start.39 = (pred[4]{0:T(512)(128)(4,1)}, pred[4]{0:T(512)(128)(4,1)S(1)}, u32[]{:S(2)}) copy-start(pred[4]{0:T(512)(128)(4,1)S(1)} %get-tuple-element.149) | copy-start | bytes 16
  12.5 7.6 %copy-start.27 = (bf16[4,3,3,64,64]{4,3,2,1,0:T(8,128)(2,1)S(1)}, bf16[4,3,3,64,64]{4,3,2,1,0:T(8,128)(2,1)}, u32[]{:S(2)}) copy-start(bf16[4,3,3,64,64]{4,3,2,1,0:T(8,128)(2,1)} %param.11) | copy-start | bytes 884740
  13.1 12.7 %collective-permute-start = (bf16[4,1,8192]{2,0,1:T(4,128)(2,1)S(1)}, bf16[4,1,8192]{2,0,1:T(4,128)(2,1)S(1)}, u32[]{:S(2)}, u32[]{:S(2)}) collective-permute-start(bf16[4,1,8192]{2,0,1:T(4,128)(2,1)S(1)} %get-tuple-element.102), channel_id=1, source_target_pairs={{0,1},{1,2},{2,3},{3,4},{4,5},{5,6},{6,7},{8,9},{9,10},{10,11},{11... | collective-permute-start | bytes 196616 | tf_op jit(solution)/shard_map/ppermute | solution.py:16
  18.0 8.6 %collective-permute-start.1 = (bf16[4,1,8192]{2,0,1:T(4,128)(2,1)S(1)}, bf16[4,1,8192]{2,0,1:T(4,128)(2,1)S(1)}, u32[]{:S(2)}, u32[]{:S(2)}) collective-permute-start(bf16[4,1,8192]{2,0,1:T(4,128)(2,1)S(1)} %get-tuple-element.103), channel_id=1, source_target_pairs={{1,0},{2,1},{3,2},{4,3},{5,4},{6,5},{7,6},{9,8},{10,9},{11,10},{12... | collective-permute-start | bytes 196616 | tf_op jit(solution)/shard_map/ppermute | solution.py:18
  21.0 2.4 copy-start.28
  32.1 8.5 %copy-start.35 = (bf16[3,64,64]{2,1,0:T(8,128)(2,1)S(1)}, bf16[3,64,64]{2,1,0:T(8,128)(2,1)}, u32[]{:S(2)}) copy-start(bf16[3,64,64]{2,1,0:T(8,128)(2,1)} %get-tuple-element.135) | copy-start | bytes 73732
  32.1 8.5 %copy-start.36 = (bf16[3,64,64]{2,1,0:T(8,128)(2,1)S(1)}, bf16[3,64,64]{2,1,0:T(8,128)(2,1)}, u32[]{:S(2)}) copy-start(bf16[3,64,64]{2,1,0:T(8,128)(2,1)} %get-tuple-element.136) | copy-start | bytes 73732
  34.5 11.2 %copy-start = (bf16[4,8,8192]{2,0,1:T(4,128)(2,1)}, bf16[4,8,8192]{2,0,1:T(4,128)(2,1)S(1)}, u32[]{:S(2)}) copy-start(bf16[4,8,8192]{2,0,1:T(4,128)(2,1)S(1)} %fusion) | copy-start | bytes 1572868
  34.6 6.4 %collective-permute-start.2 = (bf16[4,1,8192]{2,0,1:T(4,128)(2,1)S(1)}, bf16[4,1,8192]{2,0,1:T(4,128)(2,1)S(1)}, u32[]{:S(2)}, u32[]{:S(2)}) collective-permute-start(bf16[4,1,8192]{2,0,1:T(4,128)(2,1)S(1)} %get-tuple-element.100), channel_id=1, source_target_pairs={{0,1},{1,2},{2,3},{3,4},{4,5},{5,6},{6,7},{8,9},{9,10},{10,11},{11... | collective-permute-start | bytes 196616 | tf_op jit(solution)/shard_map/ppermute | solution.py:16
  39.2 6.6 %collective-permute-start.3 = (bf16[4,1,8192]{2,0,1:T(4,128)(2,1)S(1)}, bf16[4,1,8192]{2,0,1:T(4,128)(2,1)S(1)}, u32[]{:S(2)}, u32[]{:S(2)}) collective-permute-start(bf16[4,1,8192]{2,0,1:T(4,128)(2,1)S(1)} %get-tuple-element.101), channel_id=1, source_target_pairs={{1,0},{2,1},{3,2},{4,3},{5,4},{6,5},{7,6},{9,8},{10,9},{11,10},{12... | collective-permute-start | bytes 196616 | tf_op jit(solution)/shard_map/ppermute | solution.py:18
  53.5 8.5 %copy-start.61 = (u32[32]{0:T(128)S(1)}, u32[32]{0:T(128)}, u32[]{:S(2)}) copy-start(u32[32]{0:T(128)} %constant.110) | copy-start | bytes 388
  53.5 10.6 %copy-start.25 = (bf16[1,3,3,64,64]{4,3,2,1,0:T(8,128)(2,1)S(1)}, bf16[1,3,3,64,64]{4,3,2,1,0:T(8,128)(2,1)}, u32[]{:S(2)}) copy-start(bf16[1,3,3,64,64]{4,3,2,1,0:T(8,128)(2,1)} %get-tuple-element.74) | copy-start | bytes 221188
  53.5 10.8 %copy-start.26 = (bf16[1,3,3,64,64]{4,3,2,1,0:T(8,128)(2,1)S(1)}, bf16[1,3,3,64,64]{4,3,2,1,0:T(8,128)(2,1)}, u32[]{:S(2)}) copy-start(bf16[1,3,3,64,64]{4,3,2,1,0:T(8,128)(2,1)} %get-tuple-element.70) | copy-start | bytes 221188
  53.5 10.9 %copy-start.56 = (s32[4]{0:T(128)S(1)}, s32[4]{0:T(128)}, u32[]{:S(2)}) copy-start(s32[4]{0:T(128)} %get-tuple-element.28) | copy-start | bytes 52
  53.5 11.2 %copy-start.55 = (s32[4]{0:T(128)S(1)}, s32[4]{0:T(128)}, u32[]{:S(2)}) copy-start(s32[4]{0:T(128)} %get-tuple-element.27) | copy-start | bytes 52
  53.5 11.4 %copy-start.54 = (s32[4]{0:T(128)S(1)}, s32[4]{0:T(128)}, u32[]{:S(2)}) copy-start(s32[4]{0:T(128)} %get-tuple-element.25) | copy-start | bytes 52
  53.6 11.6 %copy-start.53 = (s32[4]{0:T(128)S(1)}, s32[4]{0:T(128)}, u32[]{:S(2)}) copy-start(s32[4]{0:T(128)} %get-tuple-element.26) | copy-start | bytes 52
  53.6 11.8 %copy-start.52 = (s32[4,1]{0,1:T(1,128)S(1)}, s32[4,1]{0,1:T(1,128)}, u32[]{:S(2)}) copy-start(s32[4,1]{0,1:T(1,128)} %get-tuple-element.146) | copy-start | bytes 52
  53.6 21.1 %copy-start.51 = (s32[16,2]{0,1:T(2,128)S(1)}, s32[16,2]{0,1:T(2,128)}, u32[]{:S(2)}) copy-start(s32[16,2]{0,1:T(2,128)} %param.12) | copy-start | bytes 388
  53.6 88.8 %all-gather.6.cloned.1.call-start = ((), (), s32[]{:S(2)}) async-start(), calls=%async_computation.1 | async-start | bytes 2621440 | tf_op jit(solution)/shard_map/all_gather | solution.py:149
  55.1 23.0 %copy-start.31 = (bf16[4,8,8192]{2,1,0:T(8,128)(2,1)S(1)}, bf16[4,8,8192]{2,1,0:T(8,128)(2,1)}, u32[]{:S(2)}) copy-start(bf16[4,8,8192]{2,1,0:T(8,128)(2,1)} %param.7) | copy-start | bytes 1572868
  55.1 112.0 %collective-permute-start.16 = (bf16[2,4,1,8192]{3,2,1,0:T(2,128)(2,1)}, bf16[2,4,1,8192]{3,2,1,0:T(2,128)(2,1)}, u32[]{:S(2)}, u32[]{:S(2)}) collective-permute-start(bf16[2,4,1,8192]{3,2,1,0:T(2,128)(2,1)} %get-tuple-element.54), channel_id=1, source_target_pairs={{0,1},{1,2},{2,3},{3,4},{4,5},{5,6},{6,7},{8,9},{9,10},{10,11},{11... | collective-permute-start | bytes 393224 | tf_op jit(solution)/shard_map/ppermute | solution.py:16
  60.8 106.3 %collective-permute-start.17 = (bf16[2,4,1,8192]{3,2,1,0:T(2,128)(2,1)}, bf16[2,4,1,8192]{3,2,1,0:T(2,128)(2,1)}, u32[]{:S(2)}, u32[]{:S(2)}) collective-permute-start(bf16[2,4,1,8192]{3,2,1,0:T(2,128)(2,1)} %get-tuple-element.55), channel_id=1, source_target_pairs={{1,0},{2,1},{3,2},{4,3},{5,4},{6,5},{7,6},{9,8},{10,9},{11,10},{12... | collective-permute-start | bytes 393224 | tf_op jit(solution)/shard_map/ppermute | solution.py:18
  84.2 6.7 %collective-permute-start.4 = (bf16[4,1,8192]{2,0,1:T(4,128)(2,1)S(1)}, bf16[4,1,8192]{2,0,1:T(4,128)(2,1)S(1)}, u32[]{:S(2)}, u32[]{:S(2)}) collective-permute-start(bf16[4,1,8192]{2,0,1:T(4,128)(2,1)S(1)} %get-tuple-element.98), channel_id=1, source_target_pairs={{0,1},{1,2},{2,3},{3,4},{4,5},{5,6},{6,7},{8,9},{9,10},{10,11},{11... | collective-permute-start | bytes 196616 | tf_op jit(solution)/shard_map/ppermute | solution.py:16
  87.6 6.2 %collective-permute-start.5 = (bf16[4,1,8192]{2,0,1:T(4,128)(2,1)S(1)}, bf16[4,1,8192]{2,0,1:T(4,128)(2,1)S(1)}, u32[]{:S(2)}, u32[]{:S(2)}) collective-permute-start(bf16[4,1,8192]{2,0,1:T(4,128)(2,1)S(1)} %get-tuple-element.99), channel_id=1, source_target_pairs={{1,0},{2,1},{3,2},{4,3},{5,4},{6,5},{7,6},{9,8},{10,9},{11,10},{12... | collective-permute-start | bytes 196616 | tf_op jit(solution)/shard_map/ppermute | solution.py:18
  101.7 10.5 %copy-start.2 = (bf16[4,8,8192]{2,0,1:T(4,128)(2,1)}, bf16[4,8,8192]{2,0,1:T(4,128)(2,1)S(1)}, u32[]{:S(2)}) copy-start(bf16[4,8,8192]{2,0,1:T(4,128)(2,1)S(1)} %fusion.1) | copy-start | bytes 1572868
  101.7 6.2 %collective-permute-start.6 = (bf16[4,1,8192]{2,0,1:T(4,128)(2,1)S(1)}, bf16[4,1,8192]{2,0,1:T(4,128)(2,1)S(1)}, u32[]{:S(2)}, u32[]{:S(2)}) collective-permute-start(bf16[4,1,8192]{2,0,1:T(4,128)(2,1)S(1)} %get-tuple-element.96), channel_id=1, source_target_pairs={{0,1},{1,2},{2,3},{3,4},{4,5},{5,6},{6,7},{8,9},{9,10},{10,11},{11... | collective-permute-start | bytes 196616 | tf_op jit(solution)/shard_map/ppermute | solution.py:16
  106.0 6.2 %collective-permute-start.7 = (bf16[4,1,8192]{2,0,1:T(4,128)(2,1)S(1)}, bf16[4,1,8192]{2,0,1:T(4,128)(2,1)S(1)}, u32[]{:S(2)}, u32[]{:S(2)}) collective-permute-start(bf16[4,1,8192]{2,0,1:T(4,128)(2,1)S(1)} %get-tuple-element.97), channel_id=1, source_target_pairs={{1,0},{2,1},{3,2},{4,3},{5,4},{6,5},{7,6},{9,8},{10,9},{11,10},{12... | collective-permute-start | bytes 196616 | tf_op jit(solution)/shard_map/ppermute | solution.py:18
  119.5 1.6 copy-start.21
  119.5 1.8 copy-start.23
  120.5 72.2 %all-gather.8.cloned.1.call-start = ((), (), s32[]{:S(2)}) async-start(), calls=%async_computation.2 | async-start | bytes 1310720 | tf_op jit(solution)/shard_map/all_gather | solution.py:149
  122.3 2.0 copy-start.60
  122.3 2.0 copy-start.59
  122.3 2.0 copy-start.58
  122.3 2.5 copy-start.46
  122.3 2.6 copy-start.38
  122.6 19.9 %copy-start.14 = (f32[4,8,8192]{2,0,1:T(4,128)S(1)}, f32[4,8,8192]{2,0,1:T(4,128)}, u32[]{:S(2)}) copy-start(f32[4,8,8192]{2,0,1:T(4,128)} %get-tuple-element.153) | copy-start | bytes 3145732
  142.4 10.3 %copy-start.1 = (bf16[4,8,8192]{2,0,1:T(4,128)(2,1)S(1)}, bf16[4,8,8192]{2,0,1:T(4,128)(2,1)}, u32[]{:S(2)}) copy-start(bf16[4,8,8192]{2,0,1:T(4,128)(2,1)} %copy-done) | copy-start | bytes 1572868
  148.1 6.3 %collective-permute-start.8 = (bf16[2,1,8192]{2,0,1:T(2,128)(2,1)S(1)}, bf16[2,1,8192]{2,0,1:T(2,128)(2,1)S(1)}, u32[]{:S(2)}, u32[]{:S(2)}) collective-permute-start(bf16[2,1,8192]{2,0,1:T(2,128)(2,1)S(1)} %get-tuple-element.110), channel_id=1, source_target_pairs={{0,1},{1,2},{2,3},{3,4},{4,5},{5,6},{6,7},{8,9},{9,10},{10,11},{11... | collective-permute-start | bytes 98312 | tf_op jit(solution)/shard_map/ppermute | solution.py:16
  151.5 5.8 %collective-permute-start.9 = (bf16[2,1,8192]{2,0,1:T(2,128)(2,1)S(1)}, bf16[2,1,8192]{2,0,1:T(2,128)(2,1)S(1)}, u32[]{:S(2)}, u32[]{:S(2)}) collective-permute-start(bf16[2,1,8192]{2,0,1:T(2,128)(2,1)S(1)} %get-tuple-element.111), channel_id=1, source_target_pairs={{1,0},{2,1},{3,2},{4,3},{5,4},{6,5},{7,6},{9,8},{10,9},{11,10},{12... | collective-permute-start | bytes 98312 | tf_op jit(solution)/shard_map/ppermute | solution.py:18
  159.2 7.9 %copy-start.5 = (bf16[1,4,8,8192]{3,2,1,0:T(8,128)(2,1)S(1)}, bf16[1,4,8,8192]{3,2,1,0:T(8,128)(2,1)}, u32[]{:S(2)}) copy-start(bf16[1,4,8,8192]{3,2,1,0:T(8,128)(2,1)} %get-tuple-element.94) | copy-start | bytes 1572868
  159.2 7.9 %copy-start.9 = (bf16[4,8,8192]{2,1,0:T(8,128)(2,1)S(1)}, bf16[4,8,8192]{2,1,0:T(8,128)(2,1)}, u32[]{:S(2)}) copy-start(bf16[4,8,8192]{2,1,0:T(8,128)(2,1)} %param.8) | copy-start | bytes 1572868
  161.2 10.2 %copy-start.32 = (bf16[2,8,8192]{2,0,1:T(2,128)(2,1)}, bf16[2,8,8192]{2,0,1:T(2,128)(2,1)S(1)}, u32[]{:S(2)}) copy-start(bf16[2,8,8192]{2,0,1:T(2,128)(2,1)S(1)} %fusion.2) | copy-start | bytes 786436
  161.3 7.8 %collective-permute-start.10 = (bf16[2,1,8192]{2,0,1:T(2,128)(2,1)S(1)}, bf16[2,1,8192]{2,0,1:T(2,128)(2,1)S(1)}, u32[]{:S(2)}, u32[]{:S(2)}) collective-permute-start(bf16[2,1,8192]{2,0,1:T(2,128)(2,1)S(1)} %get-tuple-element.108), channel_id=1, source_target_pairs={{0,1},{1,2},{2,3},{3,4},{4,5},{5,6},{6,7},{8,9},{9,10},{10,11},{11... | collective-permute-start | bytes 98312 | tf_op jit(solution)/shard_map/ppermute | solution.py:16
  165.6 5.8 %collective-permute-start.11 = (bf16[2,1,8192]{2,0,1:T(2,128)(2,1)S(1)}, bf16[2,1,8192]{2,0,1:T(2,128)(2,1)S(1)}, u32[]{:S(2)}, u32[]{:S(2)}) collective-permute-start(bf16[2,1,8192]{2,0,1:T(2,128)(2,1)S(1)} %get-tuple-element.109), channel_id=1, source_target_pairs={{1,0},{2,1},{3,2},{4,3},{5,4},{6,5},{7,6},{9,8},{10,9},{11,10},{12... | collective-permute-start | bytes 98312 | tf_op jit(solution)/shard_map/ppermute | solution.py:18
  176.8 197.5 %all-reduce.38.cloned.1.call-start = ((), (), s32[]{:S(2)}) async-start(), calls=%async_computation.3 | async-start | bytes 4718592 | tf_op jit(solution)/shard_map/psum | solution.py:175
  188.9 3.8 copy-start.6
  195.4 5.5 %copy-start.33 = (bf16[2,8,8192]{2,0,1:T(2,128)(2,1)S(1)}, bf16[2,8,8192]{2,0,1:T(2,128)(2,1)}, u32[]{:S(2)}) copy-start(bf16[2,8,8192]{2,0,1:T(2,128)(2,1)} %copy-done.32) | copy-start | bytes 786436
  196.0 5.7 %collective-permute-start.12 = (bf16[1,1,8192]{2,1,0:T(2,128)(2,1)S(1)}, bf16[1,1,8192]{2,1,0:T(2,128)(2,1)S(1)}, u32[]{:S(2)}, u32[]{:S(2)}) collective-permute-start(bf16[1,1,8192]{2,1,0:T(2,128)(2,1)S(1)} %get-tuple-element.142), channel_id=1, source_target_pairs={{0,1},{1,2},{2,3},{3,4},{4,5},{5,6},{6,7},{8,9},{9,10},{10,11},{11... | collective-permute-start | bytes 49160 | tf_op jit(solution)/shard_map/ppermute | solution.py:16
  199.4 5.8 %collective-permute-start.13 = (bf16[1,1,8192]{2,1,0:T(2,128)(2,1)S(1)}, bf16[1,1,8192]{2,1,0:T(2,128)(2,1)S(1)}, u32[]{:S(2)}, u32[]{:S(2)}) collective-permute-start(bf16[1,1,8192]{2,1,0:T(2,128)(2,1)S(1)} %get-tuple-element.143), channel_id=1, source_target_pairs={{1,0},{2,1},{3,2},{4,3},{5,4},{6,5},{7,6},{9,8},{10,9},{11,10},{12... | collective-permute-start | bytes 49160 | tf_op jit(solution)/shard_map/ppermute | solution.py:18
  201.6 4.3 %copy-start.29 = (bf16[3,256,128]{2,1,0:T(8,128)(2,1)S(1)}, bf16[3,256,128]{2,1,0:T(8,128)(2,1)}, u32[]{:S(2)}) copy-start(bf16[3,256,128]{2,1,0:T(8,128)(2,1)} %fusion.118) | copy-start | bytes 589828
  211.1 7.2 %collective-permute-start.14 = (bf16[1,1,8192]{2,1,0:T(2,128)(2,1)S(1)}, bf16[1,1,8192]{2,1,0:T(2,128)(2,1)S(1)}, u32[]{:S(2)}, u32[]{:S(2)}) collective-permute-start(bf16[1,1,8192]{2,1,0:T(2,128)(2,1)S(1)} %get-tuple-element.140), channel_id=1, source_target_pairs={{0,1},{1,2},{2,3},{3,4},{4,5},{5,6},{6,7},{8,9},{9,10},{10,11},{11... | collective-permute-start | bytes 49160 | tf_op jit(solution)/shard_map/ppermute | solution.py:16
  215.4 5.8 %collective-permute-start.15 = (bf16[1,1,8192]{2,1,0:T(2,128)(2,1)S(1)}, bf16[1,1,8192]{2,1,0:T(2,128)(2,1)S(1)}, u32[]{:S(2)}, u32[]{:S(2)}) collective-permute-start(bf16[1,1,8192]{2,1,0:T(2,128)(2,1)S(1)} %get-tuple-element.141), channel_id=1, source_target_pairs={{1,0},{2,1},{3,2},{4,3},{5,4},{6,5},{7,6},{9,8},{10,9},{11,10},{12... | collective-permute-start | bytes 49160 | tf_op jit(solution)/shard_map/ppermute | solution.py:18
  218.0 3.7 copy-start.30
  222.0 7.1 %copy-start.49 = (s32[4]{0:T(128)S(1)}, s32[4]{0:T(128)}, u32[]{:S(2)}) copy-start(s32[4]{0:T(128)} %get-tuple-element.19) | copy-start | bytes 52
  222.0 7.1 %copy-start.50 = (s32[4]{0:T(128)S(1)}, s32[4]{0:T(128)}, u32[]{:S(2)}) copy-start(s32[4]{0:T(128)} %get-tuple-element.20) | copy-start | bytes 52
  222.0 7.1 %copy-start.57 = (f32[4]{0:T(128)S(1)}, f32[4]{0:T(128)}, u32[]{:S(2)}) copy-start(f32[4]{0:T(128)} %convert_multiply_fusion.2) | copy-start | bytes 52
  230.6 1.8 copy-start.17
  230.6 1.8 copy-start.18
  374.3 2.5 copy-start.12
  (20 other events, 21.7 us)
Sparse Core Ops, SparseCore 0:
  53.7 24.2 all-gather.3
  120.7 21.7 all-gather.5
  176.9 15.7 all-gather.7
  238.7 135.5 all-reduce.37
where the time goes:
time: 392 us; the launch traced here: 385 us
  waiting for transfers between devices  178 us (45%)
  local copies, waits for them, and re-layouts  60 us (15%)
  starting transfers between devices  51.1 us (13%)
  matrix products  39.3 us (10%)
  other arithmetic  27.3 us (7%)
  between operations  17.3 us (4%)
  blocking collectives  12.2 us (3%)
    psum x1, waiting for transfers between devices, body_time(): weight_one, weight_two = lax.psum((sum_one, sum_two), ('tm', 'space'))  134 us
    ppermute x9, starting transfers between devices, padded_2(): lax.ppermute(tail, axis, [(i, (i + 1) % count) for i in range(ends)])  38.1 us
    ppermute x9, waiting for transfers between devices, padded_2(): lax.ppermute(head, axis, [((i + 1) % count, i) for i in range(ends)])  21.9 us
    all_gather x3, waiting for transfers between devices, body_time(): moved = lax.all_gather(to_refs, 'tm', axis=0, tiled=True)  20.7 us
    unnamed x158, local copies, waits for them, and re-layouts  18.8 us
    dot_general x4, matrix products, body_time(): jnp.einsum('kf,kx->fx', weights.astype(jnp.bfloat16), moved.reshape(moved...  14.4 us
    ppermute x9, starting transfers between devices, padded_2(): lax.ppermute(head, axis, [((i + 1) % count, i) for i in range(ends)])  12.7 us
    dot_general x4, matrix products, body_time(): jnp.einsum('sf,fx->sx', picker_wide, act_slope.reshape(frames_dev, -1), p...  9.11 us
  transfers between devices with their start and end apart: 22, of which 13 were waited for; matrix products, arithmetic and copies ran while one was open for 19% of the time, Pallas kernels for 0%

commit v1 on v0

--- a/solution.py
+++ b/solution.py
@@ -1,8 +1,18 @@
+import functools
 import math
 import jax
 import jax.numpy as jnp
 from jax import lax
 from jax.sharding import PartitionSpec as P
+
+
+def _unite_members_all(vec, shard_axis, axis_tag):
+    for t in (shard_axis, axis_tag):
+        vec = lax.psum(vec, axis_name=t)
+    return vec
+
+
+plane_convert = functools.partial(_unite_members_all, shard_axis="space", axis_tag="tm")
 
 
 def padded_2(cells, sides, width):
@@ -172,7 +182,7 @@
     scale = 1.0 / math.sqrt(row_count * lax.axis_size("space") * col_count)
     sum_one = scale * jnp.sum(level_hot[:, :, None, None, None, None] * per_one[:, None], axis=0)
     sum_two = scale * jnp.sum(level_hot[:, :, None, None, None, None] * per_two[:, None], axis=0)
-    weight_one, weight_two = lax.psum((sum_one, sum_two), ("tm", "space"))
+    weight_one, weight_two = plane_convert((sum_one, sum_two))
     return (cot_total, weight_one, weight_two)
 
 

time: 392 us -> 424 us (1.082)
  waiting for transfers between devices: 178 us -> 206 us
    psum x1 -> x2, waiting for transfers between devices: 134 us -> 164 us  [_unite_members_all(): vec = lax.psum(vec, axis_name=t)]
    unnamed x158 -> x162, local copies, waits for them, and re-layouts: 18.8 us -> 19.5 us
  transfers between devices with their start and end apart: 22 -> 23, of which waited for: 13 -> 14; matrix products, arithmetic and copies ran while one was open for 19% -> 18% of each run, Pallas kernels for 0% -> 0%
where the time goes in v1:
time: 424 us; the launch traced here: 417 us
  waiting for transfers between devices  206 us (49%)
  local copies, waits for them, and re-layouts  62.9 us (15%)
  starting transfers between devices  51.2 us (12%)
  matrix products  40.5 us (10%)
  other arithmetic  27.2 us (6%)
  between operations  17.2 us (4%)
  blocking collectives  12.2 us (3%)
    psum x2, waiting for transfers between devices, _unite_members_all(): vec = lax.psum(vec, axis_name=t)  164 us
    ppermute x9, starting transfers between devices, padded_2(): lax.ppermute(tail, axis, [(i, (i + 1) % count) for i in range(ends)])  38.1 us
    ppermute x9, waiting for transfers between devices, padded_2(): lax.ppermute(head, axis, [((i + 1) % count, i) for i in range(ends)])  21.9 us
    unnamed x162, local copies, waits for them, and re-layouts  19.5 us
    all_gather x3, waiting for transfers between devices, body_time(): moved = lax.all_gather(to_refs, 'tm', axis=0, tiled=True)  19 us
    dot_general x4, matrix products, body_time(): jnp.einsum('kf,kx->fx', weights.astype(jnp.bfloat16), moved.reshape(moved...  14.4 us
    ppermute x9, starting transfers between devices, padded_2(): lax.ppermute(head, axis, [((i + 1) % count, i) for i in range(ends)])  12.7 us
    dot_general x4, matrix products, body_time(): jnp.einsum('sf,fx->sx', picker_wide, act_slope.reshape(frames_dev, -1), p...  9.09 us
  transfers between devices with their start and end apart: 23, of which 14 were waited for; matrix products, arithmetic and copies ran while one was open for 18% of the time, Pallas kernels for 0%

profile of v1, /device:TPU:0, one launch (start us, length us, event | category | flops | bytes accessed | tf_op | source)
XLA Modules:
  0.0 416.7 jit_solution(3194860951852639385)
XLA Ops:
  7.2 1.3 broadcast_compare_fusion
  10.0 1.4 copy.215
  13.0 4.9 %collective-permute-start = (bf16[4,1,8192]{2,0,1:T(4,128)(2,1)S(1)}, bf16[4,1,8192]{2,0,1:T(4,128)(2,1)S(1)}, u32[]{:S(2)}, u32[]{:S(2)}) collective-permute-start(bf16[4,1,8192]{2,0,1:T(4,128)(2,1)S(1)} %get-tuple-element.104), channel_id=1, source_target_pairs={{0,1},{1,2},{2,3},{3,4},{4,5},{5,6},{6,7},{8,9},{9,10},{10,11},{11... | collective-permute-start | bytes 196616 | tf_op jit(solution)/shard_map/ppermute | solution.py:26
  18.0 1.3 collective-permute-start.1
  21.1 2.3 fusion.46
  27.4 1.4 select_maximum_fusion.2
  32.2 2.4 fusion
  34.6 4.5 %collective-permute-start.2 = (bf16[4,1,8192]{2,0,1:T(4,128)(2,1)S(1)}, bf16[4,1,8192]{2,0,1:T(4,128)(2,1)S(1)}, u32[]{:S(2)}, u32[]{:S(2)}) collective-permute-start(bf16[4,1,8192]{2,0,1:T(4,128)(2,1)S(1)} %get-tuple-element.102), channel_id=1, source_target_pairs={{0,1},{1,2},{2,3},{3,4},{4,5},{5,6},{6,7},{8,9},{9,10},{10,11},{11... | collective-permute-start | bytes 196616 | tf_op jit(solution)/shard_map/ppermute | solution.py:26
  39.2 1.5 collective-permute-start.3
  41.0 4.7 %collective-permute-done.3 = bf16[4,1,8192]{2,0,1:T(4,128)(2,1)S(1)} collective-permute-done((bf16[4,1,8192]{2,0,1:T(4,128)(2,1)S(1)}, bf16[4,1,8192]{2,0,1:T(4,128)(2,1)S(1)}, u32[]{:S(2)}, u32[]{:S(2)}) %collective-permute-start.3) | collective-permute-done | bytes 65568 | tf_op jit(solution)/shard_map/ppermute | solution.py:28
  46.2 1.9 reshape.439
  48.2 1.8 pad.50
  53.8 1.3 pad_maximum_fusion.21
  55.1 5.7 %collective-permute-start.16 = (bf16[2,4,1,8192]{3,2,1,0:T(2,128)(2,1)}, bf16[2,4,1,8192]{3,2,1,0:T(2,128)(2,1)}, u32[]{:S(2)}, u32[]{:S(2)}) collective-permute-start(bf16[2,4,1,8192]{3,2,1,0:T(2,128)(2,1)} %get-tuple-element.56), channel_id=1, source_target_pairs={{0,1},{1,2},{2,3},{3,4},{4,5},{5,6},{6,7},{8,9},{9,10},{10,11},{11... | collective-permute-start | bytes 393224 | tf_op jit(solution)/shard_map/ppermute | solution.py:26
  60.7 1.3 collective-permute-start.17
  66.0 1.4 dynamic-update-slice.6
  67.4 1.3 dynamic-update-slice.7
  68.7 5.6 %all-reduce.34 = (s32[16]{0:T(128)S(1)}, s32[16]{0:T(128)S(1)}, s32[16]{0:T(128)S(1)}, s32[16]{0:T(128)}, s32[8]{0:T(128)S(1)}, /*index=5*/s32[8]{0:T(128)}, s32[4]{0:T(128)S(1)}, s32[4]{0:T(128)}) all-reduce(s32[16]{0:T(128)S(1)} %dynamic-update-slice.3, s32[16]{0:T(128)S(1)} %dynamic-update-slice.1, ...), channel_id=1, replica_groups=mesh['tm'=4,'space'=8] {'tm'}, use_global_device_ids=true, to_apply=%add.29 | all-reduce | flops 88 | bytes 704
  75.4 2.6 all-gather.4.cloned.1.call-done
  78.0 5.5 %fusion.214 = (bf16[4,8,8192]{2,0,1:T(4,128)(2,1)S(1)}, f32[4,8,8192]{2,0,1:T(4,128)}) fusion(s32[16]{0:T(128)S(1)} %get-tuple-element.31, s32[16]{0:T(128)S(1)} %get-tuple-element.30, f32[16]{0:T(128)S(1)} %convert_multiply_fusion.5, s32[4]{0:T(128)S(1)} %get-tuple-element.162, bf16[4,8,8192]{2,1,0:T(8,128)(2,1)S(1)} %copy-done.31, ...), kind=kOutput, calls=%fused_computation.415 | convolution fusion | flops 9175488 | bytes 4194512 | tf_op jit(solution)/shard_map/kf,kx->fx/dot_general | solution.py:169
  84.2 3.4 collective-permute-start.4
  87.6 1.7 collective-permute-start.5
  91.7 2.0 collective-permute-done.5
  94.5 1.4 select_maximum_fusion
  99.3 2.4 fusion.1
  101.7 4.3 %collective-permute-start.6 = (bf16[4,1,8192]{2,0,1:T(4,128)(2,1)S(1)}, bf16[4,1,8192]{2,0,1:T(4,128)(2,1)S(1)}, u32[]{:S(2)}, u32[]{:S(2)}) collective-permute-start(bf16[4,1,8192]{2,0,1:T(4,128)(2,1)S(1)} %get-tuple-element.98), channel_id=1, source_target_pairs={{0,1},{1,2},{2,3},{3,4},{4,5},{5,6},{6,7},{8,9},{9,10},{10,11},{11... | collective-permute-start | bytes 196616 | tf_op jit(solution)/shard_map/ppermute | solution.py:26
  106.0 1.3 collective-permute-start.7
  107.9 4.3 %collective-permute-done.7 = bf16[4,1,8192]{2,0,1:T(4,128)(2,1)S(1)} collective-permute-done((bf16[4,1,8192]{2,0,1:T(4,128)(2,1)S(1)}, bf16[4,1,8192]{2,0,1:T(4,128)(2,1)S(1)}, u32[]{:S(2)}, u32[]{:S(2)}) %collective-permute-start.7) | collective-permute-done | bytes 65568 | tf_op jit(solution)/shard_map/ppermute | solution.py:28
  112.7 1.9 reshape.447
  114.6 1.8 pad.52
  124.8 2.4 fusion.143
  127.2 15.2 %all-gather.6.cloned.1.call-done = bf16[16,8,8192]{2,1,0:T(8,128)(2,1)} async-done(((bf16[4,8,8192]{2,1,0:T(8,128)(2,1)}), bf16[16,8,8192]{2,1,0:T(8,128)(2,1)}) %all-gather.6.cloned.1.call-update) | async-done | bytes 2097168 | tf_op jit(solution)/shard_map/all_gather | solution.py:159
  142.4 5.2 %fusion.215 = (bf16[4,8,8192]{2,0,1:T(4,128)(2,1)S(1)}, f32[4,8,8192]{2,0,1:T(4,128)}) fusion(f32[4,8,8192]{2,0,1:T(4,128)S(1)} %copy-done.14, s32[16]{0:T(128)S(1)} %get-tuple-element.32, s32[16]{0:T(128)S(1)} %get-tuple-element.29, f32[16]{0:T(128)S(1)} %convert_multiply_fusion.4, s32[4]{0:T(128)S(1)} %get-tuple-element.162, ...), kind=kOutput, calls=%fused_computation.416 | convolution fusion | flops 8913344 | bytes 4718800 | tf_op jit(solution)/shard_map/kf,kx->fx/dot_general | solution.py:169
  148.1 3.4 collective-permute-start.8
  151.5 1.3 collective-permute-start.9
  154.6 2.7 collective-permute-done.9
  159.2 2.0 fusion.2
  161.3 4.3 %collective-permute-start.10 = (bf16[2,1,8192]{2,0,1:T(2,128)(2,1)S(1)}, bf16[2,1,8192]{2,0,1:T(2,128)(2,1)S(1)}, u32[]{:S(2)}, u32[]{:S(2)}) collective-permute-start(bf16[2,1,8192]{2,0,1:T(2,128)(2,1)S(1)} %get-tuple-element.110), channel_id=1, source_target_pairs={{0,1},{1,2},{2,3},{3,4},{4,5},{5,6},{6,7},{8,9},{9,10},{10,11},{11... | collective-permute-start | bytes 98312 | tf_op jit(solution)/shard_map/ppermute | solution.py:26
  165.6 1.5 collective-permute-start.11
  167.1 2.0 pad_maximum_fusion
  169.2 2.2 collective-permute-done.11
  173.4 1.5 reshape.570
  178.5 1.9 reshape_squeeze.7
  180.4 1.8 pad.58
  184.0 1.9 reshape_squeeze.6
  185.9 1.8 pad.57
  188.6 1.3 fusion.195
  189.9 1.3 fusion.194
  192.8 2.7 fusion.216
  196.1 3.4 collective-permute-start.12
  199.4 1.5 collective-permute-start.13
  202.0 3.3 collective-permute-done.13
  211.1 4.3 %collective-permute-start.14 = (bf16[1,1,8192]{2,1,0:T(2,128)(2,1)S(1)}, bf16[1,1,8192]{2,1,0:T(2,128)(2,1)S(1)}, u32[]{:S(2)}, u32[]{:S(2)}) collective-permute-start(bf16[1,1,8192]{2,1,0:T(2,128)(2,1)S(1)} %get-tuple-element.142), channel_id=1, source_target_pairs={{0,1},{1,2},{2,3},{3,4},{4,5},{5,6},{6,7},{8,9},{9,10},{10,11},{11... | collective-permute-start | bytes 49160 | tf_op jit(solution)/shard_map/ppermute | solution.py:26
  215.4 1.3 collective-permute-start.15
  218.5 2.7 collective-permute-done.15
  222.6 6.5 %all_gather.47 = bf16[4,8,8192]{2,1,0:T(8,128)(2,1)S(1)} all-gather(bf16[1,8,8192]{2,1,0:T(8,128)(2,1)S(1)} %convert_element_type.244), channel_id=1, replica_groups=mesh['tm'=4,'space'=8] {'tm'}, dimensions={0}, use_global_device_ids=true | all-gather | bytes 655360 | tf_op jit(solution)/shard_map/all_gather | solution.py:159
  231.5 1.8 convolution_bitcast_fusion.2
  233.3 1.6 convolution_bitcast_fusion.1
  238.2 1.2 broadcast_multiply_fusion
  239.4 1.2 broadcast_multiply_fusion.1
  240.6 108.4 %all-reduce.40.cloned.1.call-done = (f32[4,3,3,64,64]{4,3,2,1,0:T(8,128)}, f32[4,3,3,64,64]{4,3,2,1,0:T(8,128)}) async-done(((f32[4,3,3,64,64]{4,3,2,1,0:T(8,128)}, f32[4,3,3,64,64]{4,3,2,1,0:T(8,128)}), (f32[4,3,3,64,64]{4,3,2,1,0:T(8,128)}, f32[4,3,3,64,64]{4,3,2,1,0:T(8,128)})) %all-reduce.40.cloned.1.call-update) | async-done | bytes 1179664 | tf_op jit(solution)/shard_map/psum | solution.py:11
  349.1 1.6 copy.155
  350.7 55.5 %all-reduce.42.cloned.1.call-done = (f32[4,3,3,64,64]{4,3,2,1,0:T(8,128)}, f32[4,3,3,64,64]{4,3,2,1,0:T(8,128)}) async-done(((f32[4,3,3,64,64]{4,3,2,1,0:T(8,128)}, f32[4,3,3,64,64]{4,3,2,1,0:T(8,128)}), (f32[4,3,3,64,64]{4,3,2,1,0:T(8,128)}, f32[4,3,3,64,64]{4,3,2,1,0:T(8,128)})) %all-reduce.42.cloned.1.call-update) | async-done | bytes 1179664 | tf_op jit(solution)/shard_map/psum | solution.py:11
  406.2 2.5 copy.334
  (344 shorter events, 67.7 us)
Async XLA Ops:
  7.2 70.9 %all-gather.4.cloned.1.call-start = ((), (), s32[]{:S(2)}) async-start(), calls=%async_computation | async-start | bytes 2621440 | tf_op jit(solution)/shard_map/all_gather | solution.py:159
  8.5 3.9 copy-start.47
  9.3 3.2 copy-start.39
  9.3 3.2 copy-start.43
  9.3 3.2 copy-start.45
  9.3 56.1 %copy-start.41 = (pred[4]{0:T(512)(128)(4,1)}, pred[4]{0:T(512)(128)(4,1)S(1)}, u32[]{:S(2)}) copy-start(pred[4]{0:T(512)(128)(4,1)S(1)} %get-tuple-element.151) | copy-start | bytes 16
  12.4 7.6 %copy-start.27 = (bf16[4,3,3,64,64]{4,3,2,1,0:T(8,128)(2,1)S(1)}, bf16[4,3,3,64,64]{4,3,2,1,0:T(8,128)(2,1)}, u32[]{:S(2)}) copy-start(bf16[4,3,3,64,64]{4,3,2,1,0:T(8,128)(2,1)} %param.11) | copy-start | bytes 884740
  13.0 12.7 %collective-permute-start = (bf16[4,1,8192]{2,0,1:T(4,128)(2,1)S(1)}, bf16[4,1,8192]{2,0,1:T(4,128)(2,1)S(1)}, u32[]{:S(2)}, u32[]{:S(2)}) collective-permute-start(bf16[4,1,8192]{2,0,1:T(4,128)(2,1)S(1)} %get-tuple-element.104), channel_id=1, source_target_pairs={{0,1},{1,2},{2,3},{3,4},{4,5},{5,6},{6,7},{8,9},{9,10},{10,11},{11... | collective-permute-start | bytes 196616 | tf_op jit(solution)/shard_map/ppermute | solution.py:26
  18.0 8.6 %collective-permute-start.1 = (bf16[4,1,8192]{2,0,1:T(4,128)(2,1)S(1)}, bf16[4,1,8192]{2,0,1:T(4,128)(2,1)S(1)}, u32[]{:S(2)}, u32[]{:S(2)}) collective-permute-start(bf16[4,1,8192]{2,0,1:T(4,128)(2,1)S(1)} %get-tuple-element.105), channel_id=1, source_target_pairs={{1,0},{2,1},{3,2},{4,3},{5,4},{6,5},{7,6},{9,8},{10,9},{11,10},{12... | collective-permute-start | bytes 196616 | tf_op jit(solution)/shard_map/ppermute | solution.py:28
  21.0 2.4 copy-start.28
  32.1 8.5 %copy-start.37 = (bf16[3,64,64]{2,1,0:T(8,128)(2,1)S(1)}, bf16[3,64,64]{2,1,0:T(8,128)(2,1)}, u32[]{:S(2)}) copy-start(bf16[3,64,64]{2,1,0:T(8,128)(2,1)} %get-tuple-element.137) | copy-start | bytes 73732
  32.1 8.5 %copy-start.38 = (bf16[3,64,64]{2,1,0:T(8,128)(2,1)S(1)}, bf16[3,64,64]{2,1,0:T(8,128)(2,1)}, u32[]{:S(2)}) copy-start(bf16[3,64,64]{2,1,0:T(8,128)(2,1)} %get-tuple-element.138) | copy-start | bytes 73732
  34.5 11.2 %copy-start = (bf16[4,8,8192]{2,0,1:T(4,128)(2,1)}, bf16[4,8,8192]{2,0,1:T(4,128)(2,1)S(1)}, u32[]{:S(2)}) copy-start(bf16[4,8,8192]{2,0,1:T(4,128)(2,1)S(1)} %fusion) | copy-start | bytes 1572868
  34.6 6.4 %collective-permute-start.2 = (bf16[4,1,8192]{2,0,1:T(4,128)(2,1)S(1)}, bf16[4,1,8192]{2,0,1:T(4,128)(2,1)S(1)}, u32[]{:S(2)}, u32[]{:S(2)}) collective-permute-start(bf16[4,1,8192]{2,0,1:T(4,128)(2,1)S(1)} %get-tuple-element.102), channel_id=1, source_target_pairs={{0,1},{1,2},{2,3},{3,4},{4,5},{5,6},{6,7},{8,9},{9,10},{10,11},{11... | collective-permute-start | bytes 196616 | tf_op jit(solution)/shard_map/ppermute | solution.py:26
  39.2 6.6 %collective-permute-start.3 = (bf16[4,1,8192]{2,0,1:T(4,128)(2,1)S(1)}, bf16[4,1,8192]{2,0,1:T(4,128)(2,1)S(1)}, u32[]{:S(2)}, u32[]{:S(2)}) collective-permute-start(bf16[4,1,8192]{2,0,1:T(4,128)(2,1)S(1)} %get-tuple-element.103), channel_id=1, source_target_pairs={{1,0},{2,1},{3,2},{4,3},{5,4},{6,5},{7,6},{9,8},{10,9},{11,10},{12... | collective-permute-start | bytes 196616 | tf_op jit(solution)/shard_map/ppermute | solution.py:28
  53.5 8.5 %copy-start.63 = (u32[32]{0:T(128)S(1)}, u32[32]{0:T(128)}, u32[]{:S(2)}) copy-start(u32[32]{0:T(128)} %constant.110) | copy-start | bytes 388
  53.5 10.4 %copy-start.25 = (bf16[1,3,3,64,64]{4,3,2,1,0:T(8,128)(2,1)S(1)}, bf16[1,3,3,64,64]{4,3,2,1,0:T(8,128)(2,1)}, u32[]{:S(2)}) copy-start(bf16[1,3,3,64,64]{4,3,2,1,0:T(8,128)(2,1)} %get-tuple-element.76) | copy-start | bytes 221188
  53.5 10.6 %copy-start.26 = (bf16[1,3,3,64,64]{4,3,2,1,0:T(8,128)(2,1)S(1)}, bf16[1,3,3,64,64]{4,3,2,1,0:T(8,128)(2,1)}, u32[]{:S(2)}) copy-start(bf16[1,3,3,64,64]{4,3,2,1,0:T(8,128)(2,1)} %get-tuple-element.72) | copy-start | bytes 221188
  53.5 10.8 %copy-start.58 = (s32[4]{0:T(128)S(1)}, s32[4]{0:T(128)}, u32[]{:S(2)}) copy-start(s32[4]{0:T(128)} %get-tuple-element.28) | copy-start | bytes 52
  53.5 11.0 %copy-start.57 = (s32[4]{0:T(128)S(1)}, s32[4]{0:T(128)}, u32[]{:S(2)}) copy-start(s32[4]{0:T(128)} %get-tuple-element.27) | copy-start | bytes 52
  53.5 11.2 %copy-start.56 = (s32[4]{0:T(128)S(1)}, s32[4]{0:T(128)}, u32[]{:S(2)}) copy-start(s32[4]{0:T(128)} %get-tuple-element.25) | copy-start | bytes 52
  53.5 11.4 %copy-start.55 = (s32[4]{0:T(128)S(1)}, s32[4]{0:T(128)}, u32[]{:S(2)}) copy-start(s32[4]{0:T(128)} %get-tuple-element.26) | copy-start | bytes 52
  53.6 11.7 %copy-start.54 = (s32[4,1]{0,1:T(1,128)S(1)}, s32[4,1]{0,1:T(1,128)}, u32[]{:S(2)}) copy-start(s32[4,1]{0,1:T(1,128)} %get-tuple-element.148) | copy-start | bytes 52
  53.6 20.8 %copy-start.53 = (s32[16,2]{0,1:T(2,128)S(1)}, s32[16,2]{0,1:T(2,128)}, u32[]{:S(2)}) copy-start(s32[16,2]{0,1:T(2,128)} %param.12) | copy-start | bytes 388
  53.6 88.8 %all-gather.6.cloned.1.call-start = ((), (), s32[]{:S(2)}) async-start(), calls=%async_computation.1 | async-start | bytes 2621440 | tf_op jit(solution)/shard_map/all_gather | solution.py:159
  55.1 23.0 %copy-start.31 = (bf16[4,8,8192]{2,1,0:T(8,128)(2,1)S(1)}, bf16[4,8,8192]{2,1,0:T(8,128)(2,1)}, u32[]{:S(2)}) copy-start(bf16[4,8,8192]{2,1,0:T(8,128)(2,1)} %param.7) | copy-start | bytes 1572868
  55.1 112.0 %collective-permute-start.16 = (bf16[2,4,1,8192]{3,2,1,0:T(2,128)(2,1)}, bf16[2,4,1,8192]{3,2,1,0:T(2,128)(2,1)}, u32[]{:S(2)}, u32[]{:S(2)}) collective-permute-start(bf16[2,4,1,8192]{3,2,1,0:T(2,128)(2,1)} %get-tuple-element.56), channel_id=1, source_target_pairs={{0,1},{1,2},{2,3},{3,4},{4,5},{5,6},{6,7},{8,9},{9,10},{10,11},{11... | collective-permute-start | bytes 393224 | tf_op jit(solution)/shard_map/ppermute | solution.py:26
  60.7 106.4 %collective-permute-start.17 = (bf16[2,4,1,8192]{3,2,1,0:T(2,128)(2,1)}, bf16[2,4,1,8192]{3,2,1,0:T(2,128)(2,1)}, u32[]{:S(2)}, u32[]{:S(2)}) collective-permute-start(bf16[2,4,1,8192]{3,2,1,0:T(2,128)(2,1)} %get-tuple-element.57), channel_id=1, source_target_pairs={{1,0},{2,1},{3,2},{4,3},{5,4},{6,5},{7,6},{9,8},{10,9},{11,10},{12... | collective-permute-start | bytes 393224 | tf_op jit(solution)/shard_map/ppermute | solution.py:28
  84.2 6.7 %collective-permute-start.4 = (bf16[4,1,8192]{2,0,1:T(4,128)(2,1)S(1)}, bf16[4,1,8192]{2,0,1:T(4,128)(2,1)S(1)}, u32[]{:S(2)}, u32[]{:S(2)}) collective-permute-start(bf16[4,1,8192]{2,0,1:T(4,128)(2,1)S(1)} %get-tuple-element.100), channel_id=1, source_target_pairs={{0,1},{1,2},{2,3},{3,4},{4,5},{5,6},{6,7},{8,9},{9,10},{10,11},{11... | collective-permute-start | bytes 196616 | tf_op jit(solution)/shard_map/ppermute | solution.py:26
  87.6 6.2 %collective-permute-start.5 = (bf16[4,1,8192]{2,0,1:T(4,128)(2,1)S(1)}, bf16[4,1,8192]{2,0,1:T(4,128)(2,1)S(1)}, u32[]{:S(2)}, u32[]{:S(2)}) collective-permute-start(bf16[4,1,8192]{2,0,1:T(4,128)(2,1)S(1)} %get-tuple-element.101), channel_id=1, source_target_pairs={{1,0},{2,1},{3,2},{4,3},{5,4},{6,5},{7,6},{9,8},{10,9},{11,10},{12... | collective-permute-start | bytes 196616 | tf_op jit(solution)/shard_map/ppermute | solution.py:28
  101.7 10.5 %copy-start.2 = (bf16[4,8,8192]{2,0,1:T(4,128)(2,1)}, bf16[4,8,8192]{2,0,1:T(4,128)(2,1)S(1)}, u32[]{:S(2)}) copy-start(bf16[4,8,8192]{2,0,1:T(4,128)(2,1)S(1)} %fusion.1) | copy-start | bytes 1572868
  101.7 6.2 %collective-permute-start.6 = (bf16[4,1,8192]{2,0,1:T(4,128)(2,1)S(1)}, bf16[4,1,8192]{2,0,1:T(4,128)(2,1)S(1)}, u32[]{:S(2)}, u32[]{:S(2)}) collective-permute-start(bf16[4,1,8192]{2,0,1:T(4,128)(2,1)S(1)} %get-tuple-element.98), channel_id=1, source_target_pairs={{0,1},{1,2},{2,3},{3,4},{4,5},{5,6},{6,7},{8,9},{9,10},{10,11},{11... | collective-permute-start | bytes 196616 | tf_op jit(solution)/shard_map/ppermute | solution.py:26
  106.0 6.2 %collective-permute-start.7 = (bf16[4,1,8192]{2,0,1:T(4,128)(2,1)S(1)}, bf16[4,1,8192]{2,0,1:T(4,128)(2,1)S(1)}, u32[]{:S(2)}, u32[]{:S(2)}) collective-permute-start(bf16[4,1,8192]{2,0,1:T(4,128)(2,1)S(1)} %get-tuple-element.99), channel_id=1, source_target_pairs={{1,0},{2,1},{3,2},{4,3},{5,4},{6,5},{7,6},{9,8},{10,9},{11,10},{12... | collective-permute-start | bytes 196616 | tf_op jit(solution)/shard_map/ppermute | solution.py:28
  119.5 1.8 copy-start.23
  120.6 72.2 %all-gather.8.cloned.1.call-start = ((), (), s32[]{:S(2)}) async-start(), calls=%async_computation.2 | async-start | bytes 1310720 | tf_op jit(solution)/shard_map/all_gather | solution.py:159
  122.2 2.0 copy-start.62
  122.3 2.0 copy-start.61
  122.3 2.0 copy-start.60
  122.3 2.5 copy-start.48
  122.3 2.5 copy-start.40
  122.6 19.9 %copy-start.14 = (f32[4,8,8192]{2,0,1:T(4,128)S(1)}, f32[4,8,8192]{2,0,1:T(4,128)}, u32[]{:S(2)}) copy-start(f32[4,8,8192]{2,0,1:T(4,128)} %get-tuple-element.155) | copy-start | bytes 3145732
  142.4 10.3 %copy-start.1 = (bf16[4,8,8192]{2,0,1:T(4,128)(2,1)S(1)}, bf16[4,8,8192]{2,0,1:T(4,128)(2,1)}, u32[]{:S(2)}) copy-start(bf16[4,8,8192]{2,0,1:T(4,128)(2,1)} %copy-done) | copy-start | bytes 1572868
  148.1 6.4 %collective-permute-start.8 = (bf16[2,1,8192]{2,0,1:T(2,128)(2,1)S(1)}, bf16[2,1,8192]{2,0,1:T(2,128)(2,1)S(1)}, u32[]{:S(2)}, u32[]{:S(2)}) collective-permute-start(bf16[2,1,8192]{2,0,1:T(2,128)(2,1)S(1)} %get-tuple-element.112), channel_id=1, source_target_pairs={{0,1},{1,2},{2,3},{3,4},{4,5},{5,6},{6,7},{8,9},{9,10},{10,11},{11... | collective-permute-start | bytes 98312 | tf_op jit(solution)/shard_map/ppermute | solution.py:26
  151.5 5.8 %collective-permute-start.9 = (bf16[2,1,8192]{2,0,1:T(2,128)(2,1)S(1)}, bf16[2,1,8192]{2,0,1:T(2,128)(2,1)S(1)}, u32[]{:S(2)}, u32[]{:S(2)}) collective-permute-start(bf16[2,1,8192]{2,0,1:T(2,128)(2,1)S(1)} %get-tuple-element.113), channel_id=1, source_target_pairs={{1,0},{2,1},{3,2},{4,3},{5,4},{6,5},{7,6},{9,8},{10,9},{11,10},{12... | collective-permute-start | bytes 98312 | tf_op jit(solution)/shard_map/ppermute | solution.py:28
  159.2 7.9 %copy-start.5 = (bf16[1,4,8,8192]{3,2,1,0:T(8,128)(2,1)S(1)}, bf16[1,4,8,8192]{3,2,1,0:T(8,128)(2,1)}, u32[]{:S(2)}) copy-start(bf16[1,4,8,8192]{3,2,1,0:T(8,128)(2,1)} %get-tuple-element.96) | copy-start | bytes 1572868
  159.2 7.9 %copy-start.9 = (bf16[4,8,8192]{2,1,0:T(8,128)(2,1)S(1)}, bf16[4,8,8192]{2,1,0:T(8,128)(2,1)}, u32[]{:S(2)}) copy-start(bf16[4,8,8192]{2,1,0:T(8,128)(2,1)} %param.8) | copy-start | bytes 1572868
  161.2 10.2 %copy-start.34 = (bf16[2,8,8192]{2,0,1:T(2,128)(2,1)}, bf16[2,8,8192]{2,0,1:T(2,128)(2,1)S(1)}, u32[]{:S(2)}) copy-start(bf16[2,8,8192]{2,0,1:T(2,128)(2,1)S(1)} %fusion.2) | copy-start | bytes 786436
  161.3 7.9 %collective-permute-start.10 = (bf16[2,1,8192]{2,0,1:T(2,128)(2,1)S(1)}, bf16[2,1,8192]{2,0,1:T(2,128)(2,1)S(1)}, u32[]{:S(2)}, u32[]{:S(2)}) collective-permute-start(bf16[2,1,8192]{2,0,1:T(2,128)(2,1)S(1)} %get-tuple-element.110), channel_id=1, source_target_pairs={{0,1},{1,2},{2,3},{3,4},{4,5},{5,6},{6,7},{8,9},{9,10},{10,11},{11... | collective-permute-start | bytes 98312 | tf_op jit(solution)/shard_map/ppermute | solution.py:26
  165.6 5.8 %collective-permute-start.11 = (bf16[2,1,8192]{2,0,1:T(2,128)(2,1)S(1)}, bf16[2,1,8192]{2,0,1:T(2,128)(2,1)S(1)}, u32[]{:S(2)}, u32[]{:S(2)}) collective-permute-start(bf16[2,1,8192]{2,0,1:T(2,128)(2,1)S(1)} %get-tuple-element.111), channel_id=1, source_target_pairs={{1,0},{2,1},{3,2},{4,3},{5,4},{6,5},{7,6},{9,8},{10,9},{11,10},{12... | collective-permute-start | bytes 98312 | tf_op jit(solution)/shard_map/ppermute | solution.py:28
  176.8 172.2 %all-reduce.40.cloned.1.call-start = ((), (), s32[]{:S(2)}) async-start(), calls=%async_computation.3 | async-start | bytes 4718592 | tf_op jit(solution)/shard_map/psum | solution.py:11
  195.5 5.5 %copy-start.35 = (bf16[2,8,8192]{2,0,1:T(2,128)(2,1)S(1)}, bf16[2,8,8192]{2,0,1:T(2,128)(2,1)}, u32[]{:S(2)}) copy-start(bf16[2,8,8192]{2,0,1:T(2,128)(2,1)} %copy-done.34) | copy-start | bytes 786436
  196.1 5.7 %collective-permute-start.12 = (bf16[1,1,8192]{2,1,0:T(2,128)(2,1)S(1)}, bf16[1,1,8192]{2,1,0:T(2,128)(2,1)S(1)}, u32[]{:S(2)}, u32[]{:S(2)}) collective-permute-start(bf16[1,1,8192]{2,1,0:T(2,128)(2,1)S(1)} %get-tuple-element.144), channel_id=1, source_target_pairs={{0,1},{1,2},{2,3},{3,4},{4,5},{5,6},{6,7},{8,9},{9,10},{10,11},{11... | collective-permute-start | bytes 49160 | tf_op jit(solution)/shard_map/ppermute | solution.py:26
  199.4 5.8 %collective-permute-start.13 = (bf16[1,1,8192]{2,1,0:T(2,128)(2,1)S(1)}, bf16[1,1,8192]{2,1,0:T(2,128)(2,1)S(1)}, u32[]{:S(2)}, u32[]{:S(2)}) collective-permute-start(bf16[1,1,8192]{2,1,0:T(2,128)(2,1)S(1)} %get-tuple-element.145), channel_id=1, source_target_pairs={{1,0},{2,1},{3,2},{4,3},{5,4},{6,5},{7,6},{9,8},{10,9},{11,10},{12... | collective-permute-start | bytes 49160 | tf_op jit(solution)/shard_map/ppermute | solution.py:28
  201.6 4.3 %copy-start.29 = (bf16[3,256,128]{2,1,0:T(8,128)(2,1)S(1)}, bf16[3,256,128]{2,1,0:T(8,128)(2,1)}, u32[]{:S(2)}) copy-start(bf16[3,256,128]{2,1,0:T(8,128)(2,1)} %fusion.118) | copy-start | bytes 589828
  211.1 7.2 %collective-permute-start.14 = (bf16[1,1,8192]{2,1,0:T(2,128)(2,1)S(1)}, bf16[1,1,8192]{2,1,0:T(2,128)(2,1)S(1)}, u32[]{:S(2)}, u32[]{:S(2)}) collective-permute-start(bf16[1,1,8192]{2,1,0:T(2,128)(2,1)S(1)} %get-tuple-element.142), channel_id=1, source_target_pairs={{0,1},{1,2},{2,3},{3,4},{4,5},{5,6},{6,7},{8,9},{9,10},{10,11},{11... | collective-permute-start | bytes 49160 | tf_op jit(solution)/shard_map/ppermute | solution.py:26
  215.4 5.8 %collective-permute-start.15 = (bf16[1,1,8192]{2,1,0:T(2,128)(2,1)S(1)}, bf16[1,1,8192]{2,1,0:T(2,128)(2,1)S(1)}, u32[]{:S(2)}, u32[]{:S(2)}) collective-permute-start(bf16[1,1,8192]{2,1,0:T(2,128)(2,1)S(1)} %get-tuple-element.143), channel_id=1, source_target_pairs={{1,0},{2,1},{3,2},{4,3},{5,4},{6,5},{7,6},{9,8},{10,9},{11,10},{12... | collective-permute-start | bytes 49160 | tf_op jit(solution)/shard_map/ppermute | solution.py:28
  218.1 3.7 copy-start.30
  222.1 7.1 %copy-start.51 = (s32[4]{0:T(128)S(1)}, s32[4]{0:T(128)}, u32[]{:S(2)}) copy-start(s32[4]{0:T(128)} %get-tuple-element.19) | copy-start | bytes 52
  222.1 7.1 %copy-start.52 = (s32[4]{0:T(128)S(1)}, s32[4]{0:T(128)}, u32[]{:S(2)}) copy-start(s32[4]{0:T(128)} %get-tuple-element.20) | copy-start | bytes 52
  222.1 7.1 %copy-start.59 = (f32[4]{0:T(128)S(1)}, f32[4]{0:T(128)}, u32[]{:S(2)}) copy-start(f32[4]{0:T(128)} %convert_multiply_fusion.2) | copy-start | bytes 52
  231.5 1.8 copy-start.17
  231.5 1.8 copy-start.18
  240.6 165.6 %all-reduce.42.cloned.1.call-start = ((), (), s32[]{:S(2)}) async-start(), calls=%async_computation.4 | async-start | bytes 4718592 | tf_op jit(solution)/shard_map/psum | solution.py:11
  406.2 2.5 copy-start.12
  (23 other events, 26.7 us)
Sparse Core Ops, SparseCore 0:
  53.7 24.2 all-gather.3
  120.7 21.6 all-gather.5
  177.0 15.7 all-gather.7
  240.7 108.3 all-reduce.39
  351.3 54.8 all-reduce.41
